TPU v7x, 32 devices: a whole 2x2x4 slice. The times are simulated.
32 devices in a mesh: groups: 2 (over y), shard: 16 (over z, x, core).
Axes of the slice: x: 2, y: 2, z: 4, core: 2. Of those that a mesh axis runs over, the one named last changes fastest.
Arguments:
- query_tokens: bfloat16 [1024, 32, 128], P(('groups', 'shard')), parts along dimension 0, may hold values from -0.1875 to 0.1875
- candidates: int32 [1024, 24], P(('groups', 'shard')), parts along dimension 0, may hold values from 0 to 511, as said below
- cand_count: int32 [1024], P(('groups', 'shard')), parts along dimension 0, may hold values from 3 to 24, as said below
- placement_map: int32 [1024], P('groups'), parts along dimension 0, may hold values from 0 to 511, as said below
- passage_base: bfloat16 [1024, 128, 128], P(('groups', 'shard')), parts along dimension 0, may hold values from -6 to 6
- residual_codes: int32 [1024, 128, 128], P(('groups', 'shard')), parts along dimension 0, may hold values from 0 to 3
- passage_lengths: int32 [1024], P(('groups', 'shard')), parts along dimension 0, may hold values from 32 to 128
- bucket_weights: float32 [8], P('groups'), parts along dimension 0, may hold values from -3 to 3
Outputs:
- scores: float32 [1024, 24], P(('groups', 'shard')), parts along dimension 0
There are 2 independent parts, one for each index of `groups`. A program takes and returns all parts, laid end to end along the dimension named above; each array names one. Nothing has to cross between parts.
Inputs may be any that keep to these rules, and one draw needn't show every extreme that they name: In row q the first cand_count[q] entries are distinct passage ids; the devices that store them (device placement_map[id] // 32 of the shard axis) are at most 3, and one device stores at most 8 of them. Of the 32 queries of one device, one storing device (the same for all devices) holds candidates of exactly 9, and every other storing device holds candidates of at most 6. Entries at or beyond cand_count[q] are arbitrary ids. `cand_count`: entries of candidates at or beyond this count are not scored. A permutation: passage id p is row placement_map[p] of the passage store.
All inputs are finite; a program needn't handle non-finite values.
Results may differ from a plain program's by a relative error of at most 0.0003.
Values may be sent and summed in bfloat16 or wider, within the bound.
A program may use at most 64 MiB of HBM per device.

v0:
```python
import jax
import jax.numpy as jnp
from jax import lax
from jax.sharding import PartitionSpec as P

OWNERS_Q = 3
CPQ = 8


epsilon = 1e-06
negative = -1e30


def decode(bases, code_ids, levels):
    residual = jnp.zeros(bases.shape, jnp.float32)
    for bucket in range(4):
        residual = residual + jnp.where(code_ids == bucket, levels[bucket], 0.0)
    summed = bases.astype(jnp.float32) + residual
    inverse_norm = lax.rsqrt(jnp.sum(summed * summed, axis=-1, keepdims=True) + epsilon)
    return (summed * inverse_norm).astype(jnp.bfloat16)


def score_block(query_rows, token_rows, lengths):
    similarity_scores = jnp.einsum(
        "mqd,mkpd->mqkp", query_rows, token_rows, preferred_element_type=jnp.float32
    )
    inside = (
        jnp.arange(token_rows.shape[2], dtype=jnp.int32)[None, None, None, :]
        < lengths[:, None, :, None]
    )
    maxima = jnp.max(jnp.where(inside, similarity_scores, negative), axis=3)
    return jnp.sum(maxima, axis=1)


def score_slots(query_rows, wanted, decoded, lengths):
    item_count = query_rows.shape[0]
    group_size = 16
    padding = -item_count % group_size
    wanted = jnp.maximum(wanted, 0)
    blocks = (item_count + padding) // group_size

    def one_block(bundle):
        query_part, row_part = bundle
        return score_block(query_part, decoded[row_part], lengths[row_part])

    result = lax.map(
        one_block,
        (
            query_rows.reshape(blocks, group_size, query_rows.shape[1], query_rows.shape[2]),
            wanted.reshape(blocks, group_size, wanted.shape[1]),
        ),
    )
    return result.reshape(blocks * group_size, wanted.shape[1])


def pack(present, holder, capacity, query_tokens):
    present_int = present.astype(jnp.int32)
    slot_of = jnp.cumsum(present_int, axis=0) - present_int
    selection_mask = present.T[:, None, :] & (
        slot_of.T[:, None, :] == jnp.arange(capacity, dtype=jnp.int32)[None, :, None]
    )
    outgoing = jnp.einsum(
        "ksq,qtd->kstd",
        selection_mask.astype(jnp.bfloat16),
        query_tokens,
        preferred_element_type=jnp.float32,
    ).astype(jnp.bfloat16)
    target = (
        jnp.sum(
            selection_mask[:, :, :, None].astype(jnp.int32)
            * (jnp.transpose(holder, (1, 0, 2))[:, None, :, :] + 1),
            axis=2,
        )
        - 1
    )
    return (outgoing, target, slot_of)


def local(
    query_tokens,
    candidates,
    cand_count,
    placement_map,
    passage_base,
    residual_codes,
    passage_lengths,
    bucket_weights,
):
    device_count = lax.axis_size("shard")
    query_count, slot_count = candidates.shape
    store_rows = passage_base.shape[0]
    hot_cap = query_count * OWNERS_Q // device_count + 3
    decoded = decode(passage_base, residual_codes, bucket_weights)
    usable = jnp.arange(slot_count, dtype=jnp.int32)[None, :] < cand_count[:, None]
    stored = placement_map[candidates]
    holders = stored // store_rows
    local_row = stored % store_rows
    shared = usable[:, :, None] & usable[:, None, :] & (holders[:, :, None] == holders[:, None, :])
    preceding_total = (
        jnp.arange(slot_count, dtype=jnp.int32)[None, :]
        < jnp.arange(slot_count, dtype=jnp.int32)[:, None]
    )
    within = jnp.sum((shared & preceding_total[None, :, :]).astype(jnp.int32), axis=2)
    owner_ids = jnp.arange(device_count, dtype=jnp.int32)
    matches = usable[:, :, None] & (holders[:, :, None] == owner_ids[None, None, :])
    present = jnp.any(matches, axis=1)
    rank_ids = jnp.arange(CPQ, dtype=jnp.int32)
    holder = (
        jnp.sum(
            jnp.where(
                matches[:, :, :, None]
                & (within[:, :, None, None] == rank_ids[None, None, None, :]),
                local_row[:, :, None, None] + 1,
                0,
            ),
            axis=1,
        )
        - 1
    )
    outgoing, target, slot_of = pack(present, holder, hot_cap, query_tokens)
    queries_in = lax.all_to_all(outgoing, "shard", split_axis=0, concat_axis=0, tiled=True)
    rows_in = lax.all_to_all(
        target.astype(jnp.bfloat16), "shard", split_axis=0, concat_axis=0, tiled=True
    )
    senders = rows_in.shape[0]
    slots_in = rows_in.shape[1]
    flat_queries = queries_in.reshape(senders * slots_in, queries_in.shape[2], queries_in.shape[3])
    row_list_flat = rows_in.astype(jnp.int32).reshape(senders * slots_in, rows_in.shape[2])
    visited = score_slots(flat_queries, row_list_flat, decoded, passage_lengths).reshape(
        senders, slots_in, rows_in.shape[2]
    )
    returned = lax.all_to_all(visited, "shard", split_axis=0, concat_axis=0, tiled=True)
    flattened = returned.reshape(-1)
    pick_slot = jnp.take_along_axis(slot_of, jnp.clip(holders, 0, device_count - 1), axis=1)
    position = holders * (hot_cap * CPQ) + pick_slot * CPQ + within
    result = jnp.take(flattened, position, mode="clip")
    return jnp.where(usable, result, 0.0)


def solution(mesh):
    return jax.shard_map(
        local,
        mesh=mesh,
        in_specs=(
            P(("groups", "shard"), None, None),
            P(("groups", "shard"), None),
            P(("groups", "shard")),
            P("groups"),
            P(("groups", "shard"), None, None),
            P(("groups", "shard"), None, None),
            P(("groups", "shard")),
            P("groups"),
        ),
        out_specs=P(("groups", "shard"), None),
        check_vma=False,
    )
```

profile of v0, /device:TPU:0, one launch (start us, length us, event | category | flops | bytes accessed | tf_op | source)
XLA Modules:
  0.0 154.1 jit_solution(14491903596649840008)
XLA Ops:
  1.8 5.0 %gather_fusion.2 = s32[768]{0:T(1024)S(1)} fusion(s32[512]{0:T(512)S(1)} %copy-done, s32[1024]{0:T(1024)S(1)} %pad_clamp_fusion.2), kind=kCustom, calls=%fused_computation.2 | custom fusion | bytes 9216 | tf_op jit(solution)/shard_map/gather | solution.py:95
  11.2 7.4 %all-to-all-start = ((bf16[16,9,8]{1,2,0:T(8,128)(2,1)}), bf16[16,9,8]{1,2,0:T(8,128)(2,1)S(1)}, u32[]{:S(2)}, u32[]{:S(2)}) async-start(bf16[16,9,8]{1,2,0:T(8,128)(2,1)} %copy.114), calls=%async_computation | async-start | bytes 65536 | tf_op jit(solution)/shard_map/all_to_all | solution.py:122
  20.4 4.9 %all-to-all-done = bf16[16,9,8]{1,2,0:T(8,128)(2,1)S(1)} async-done(((bf16[16,9,8]{1,2,0:T(8,128)(2,1)}), bf16[16,9,8]{1,2,0:T(8,128)(2,1)S(1)}, u32[]{:S(2)}, u32[]{:S(2)}) %all-to-all-start) | async-done | bytes 2336 | tf_op jit(solution)/shard_map/all_to_all | solution.py:122
  25.2 4.4 %all-to-all-start.1 = ((bf16[16,9,32,128]{3,2,1,0:T(8,128)(2,1)}), bf16[16,9,32,128]{3,2,1,0:T(8,128)(2,1)}, u32[]{:S(2)}, u32[]{:S(2)}) async-start(bf16[16,9,32,128]{3,2,1,0:T(8,128)(2,1)} %copy.118), calls=%async_computation.1 | async-start | bytes 2359296 | tf_op jit(solution)/shard_map/all_to_all | solution.py:121
  30.0 5.1 %gather_fusion.4 = s32[768]{0:T(1024)S(1)} fusion(s32[32,16]{1,0:T(8,128)S(1)} %convert_subtract_fusion, s32[768]{0:T(1024)S(1)} %reshape.292), kind=kCustom, calls=%fused_computation.4 | custom fusion | bytes 12288 | tf_op jit(solution)/shard_map/jit(take_along_axis)/gather | solution.py:134
  36.2 4.8 %multiply_reduce_fusion = f32[32,128]{1,0:T(8,128)S(1)} fusion(f32[]{:T(128)} %bitcast.17, s32[32,128,128]{2,1,0:T(8,128)S(1)} %copy-done.2, f32[]{:T(128)} %bitcast.16, f32[]{:T(128)} %bitcast.15, f32[]{:T(128)} %bitcast.14, bf16[32,128,128]{2,1,0:T(8,128)(2,1)} %param.14), kind=kLoop, calls=%fused_computation.14 | loop fusion | flops 7860224 | bytes 3162128 | tf_op jit(solution)/shard_map/reduce_sum | solution.py:19
  41.0 4.6 %multiply_convert_fusion = bf16[32,128,128]{2,1,0:T(8,128)(2,1)S(1)} fusion(f32[32,128]{1,0:T(8,128)S(1)} %add_rsqrt_fusion, f32[]{:T(128)} %bitcast.17, s32[32,128,128]{2,1,0:T(8,128)S(1)} %copy-done.2, f32[]{:T(128)} %bitcast.16, f32[]{:T(128)} %bitcast.15, f32[]{:T(128)} %bitcast.14, bf16[32,128,128]{2,1,0:T(8,128)(2,1)} %param.14), kind=kLoop, calls=%fused_computation.13 | loop fusion | flops 7864320 | bytes 4210704 | tf_op jit(solution)/shard_map/convert_element_type | solution.py:20
  46.0 8.7 %all-to-all-done.1 = bf16[16,9,32,128]{3,2,1,0:T(8,128)(2,1)} async-done(((bf16[16,9,32,128]{3,2,1,0:T(8,128)(2,1)}), bf16[16,9,32,128]{3,2,1,0:T(8,128)(2,1)}, u32[]{:S(2)}, u32[]{:S(2)}) %all-to-all-start.1) | async-done | bytes 1179680 | tf_op jit(solution)/shard_map/all_to_all | solution.py:121
  54.7 78.7 %while.10 = (s32[]{:T(128)}, f32[9,16,8]{1,0,2:T(8,128)S(1)}, s32[9,16,8]{1,0,2:T(8,128)S(1)}, s32[32]{0:T(128)S(1)}, bf16[9,16,32,128]{3,2,1,0:T(8,128)(2,1)}, ...) while((s32[]{:T(128)}, f32[9,16,8]{1,0,2:T(8,128)S(1)}, ...), condition=%wide.region_9.10_spmd, body=%wide.region_6.9_spmd.sunk | while | flops 135283968 | bytes 12794485 | solution.py:46
  56.3 3.0 %gather_fusion = bf16[128,128,128]{2,1,0:T(8,128)(2,1)} fusion(bf16[32,128,128]{2,1,0:T(8,128)(2,1)S(1)} %get-tuple-element.148, s32[1024]{0:T(1024)S(1)} %pad_clamp_fusion.4), kind=kCustom, calls=%fused_computation.1.clone.1 | custom fusion | bytes 8389120 | tf_op jit(solution)/shard_map/while/body/eval_jaxpr/gather | solution.py:44
  59.3 3.9 %select_reduce_fusion.3 = f32[16,32,8]{1,2,0:T(8,128)S(1)} fusion(bf16[16,8,128,128]{3,2,1,0:T(8,128)(2,1)} %bitcast.55, pred[16,8,128]{2,1,0:T(8,128)(4,1)S(1)} %iota_compare_fusion.7, bf16[9,16,32,128]{3,2,1,0:T(8,128)(2,1)} %get-tuple-element.147, s32[]{:T(128)S(6)} %copy.149), kind=kOutput, calls=%fused_computation.5.clone.1 | convolution fusion | flops 135262208 | bytes 4358148 | tf_op jit(solution)/shard_map/while/body/eval_jaxpr/mqd,mkpd->mqkp/dot_general | solution.py:24
  68.1 3.9 %select_reduce_fusion.3 = f32[16,32,8]{1,2,0:T(8,128)S(1)} fusion(bf16[16,8,128,128]{3,2,1,0:T(8,128)(2,1)} %bitcast.55, pred[16,8,128]{2,1,0:T(8,128)(4,1)S(1)} %iota_compare_fusion.7, bf16[9,16,32,128]{3,2,1,0:T(8,128)(2,1)} %get-tuple-element.147, s32[]{:T(128)S(6)} %copy.149), kind=kOutput, calls=%fused_computation.5.clone.1 | convolution fusion | flops 135262208 | bytes 4358148 | tf_op jit(solution)/shard_map/while/body/eval_jaxpr/mqd,mkpd->mqkp/dot_general | solution.py:24
  73.8 3.0 %gather_fusion = bf16[128,128,128]{2,1,0:T(8,128)(2,1)} fusion(bf16[32,128,128]{2,1,0:T(8,128)(2,1)S(1)} %get-tuple-element.148, s32[1024]{0:T(1024)S(1)} %pad_clamp_fusion.4), kind=kCustom, calls=%fused_computation.1.clone.1 | custom fusion | bytes 8389120 | tf_op jit(solution)/shard_map/while/body/eval_jaxpr/gather | solution.py:44
  76.8 3.9 %select_reduce_fusion.3 = f32[16,32,8]{1,2,0:T(8,128)S(1)} fusion(bf16[16,8,128,128]{3,2,1,0:T(8,128)(2,1)} %bitcast.55, pred[16,8,128]{2,1,0:T(8,128)(4,1)S(1)} %iota_compare_fusion.7, bf16[9,16,32,128]{3,2,1,0:T(8,128)(2,1)} %get-tuple-element.147, s32[]{:T(128)S(6)} %copy.149), kind=kOutput, calls=%fused_computation.5.clone.1 | convolution fusion | flops 135262208 | bytes 4358148 | tf_op jit(solution)/shard_map/while/body/eval_jaxpr/mqd,mkpd->mqkp/dot_general | solution.py:24
  85.6 3.9 %select_reduce_fusion.3 = f32[16,32,8]{1,2,0:T(8,128)S(1)} fusion(bf16[16,8,128,128]{3,2,1,0:T(8,128)(2,1)} %bitcast.55, pred[16,8,128]{2,1,0:T(8,128)(4,1)S(1)} %iota_compare_fusion.7, bf16[9,16,32,128]{3,2,1,0:T(8,128)(2,1)} %get-tuple-element.147, s32[]{:T(128)S(6)} %copy.149), kind=kOutput, calls=%fused_computation.5.clone.1 | convolution fusion | flops 135262208 | bytes 4358148 | tf_op jit(solution)/shard_map/while/body/eval_jaxpr/mqd,mkpd->mqkp/dot_general | solution.py:24
  94.3 3.9 %select_reduce_fusion.3 = f32[16,32,8]{1,2,0:T(8,128)S(1)} fusion(bf16[16,8,128,128]{3,2,1,0:T(8,128)(2,1)} %bitcast.55, pred[16,8,128]{2,1,0:T(8,128)(4,1)S(1)} %iota_compare_fusion.7, bf16[9,16,32,128]{3,2,1,0:T(8,128)(2,1)} %get-tuple-element.147, s32[]{:T(128)S(6)} %copy.149), kind=kOutput, calls=%fused_computation.5.clone.1 | convolution fusion | flops 135262208 | bytes 4358148 | tf_op jit(solution)/shard_map/while/body/eval_jaxpr/mqd,mkpd->mqkp/dot_general | solution.py:24
  103.1 3.9 %select_reduce_fusion.3 = f32[16,32,8]{1,2,0:T(8,128)S(1)} fusion(bf16[16,8,128,128]{3,2,1,0:T(8,128)(2,1)} %bitcast.55, pred[16,8,128]{2,1,0:T(8,128)(4,1)S(1)} %iota_compare_fusion.7, bf16[9,16,32,128]{3,2,1,0:T(8,128)(2,1)} %get-tuple-element.147, s32[]{:T(128)S(6)} %copy.149), kind=kOutput, calls=%fused_computation.5.clone.1 | convolution fusion | flops 135262208 | bytes 4358148 | tf_op jit(solution)/shard_map/while/body/eval_jaxpr/mqd,mkpd->mqkp/dot_general | solution.py:24
  108.8 3.0 %gather_fusion = bf16[128,128,128]{2,1,0:T(8,128)(2,1)} fusion(bf16[32,128,128]{2,1,0:T(8,128)(2,1)S(1)} %get-tuple-element.148, s32[1024]{0:T(1024)S(1)} %pad_clamp_fusion.4), kind=kCustom, calls=%fused_computation.1.clone.1 | custom fusion | bytes 8389120 | tf_op jit(solution)/shard_map/while/body/eval_jaxpr/gather | solution.py:44
  111.8 3.9 %select_reduce_fusion.3 = f32[16,32,8]{1,2,0:T(8,128)S(1)} fusion(bf16[16,8,128,128]{3,2,1,0:T(8,128)(2,1)} %bitcast.55, pred[16,8,128]{2,1,0:T(8,128)(4,1)S(1)} %iota_compare_fusion.7, bf16[9,16,32,128]{3,2,1,0:T(8,128)(2,1)} %get-tuple-element.147, s32[]{:T(128)S(6)} %copy.149), kind=kOutput, calls=%fused_computation.5.clone.1 | convolution fusion | flops 135262208 | bytes 4358148 | tf_op jit(solution)/shard_map/while/body/eval_jaxpr/mqd,mkpd->mqkp/dot_general | solution.py:24
  120.6 3.9 %select_reduce_fusion.3 = f32[16,32,8]{1,2,0:T(8,128)S(1)} fusion(bf16[16,8,128,128]{3,2,1,0:T(8,128)(2,1)} %bitcast.55, pred[16,8,128]{2,1,0:T(8,128)(4,1)S(1)} %iota_compare_fusion.7, bf16[9,16,32,128]{3,2,1,0:T(8,128)(2,1)} %get-tuple-element.147, s32[]{:T(128)S(6)} %copy.149), kind=kOutput, calls=%fused_computation.5.clone.1 | convolution fusion | flops 135262208 | bytes 4358148 | tf_op jit(solution)/shard_map/while/body/eval_jaxpr/mqd,mkpd->mqkp/dot_general | solution.py:24
  129.3 3.9 %select_reduce_fusion.3 = f32[16,32,8]{1,2,0:T(8,128)S(1)} fusion(bf16[16,8,128,128]{3,2,1,0:T(8,128)(2,1)} %bitcast.55, pred[16,8,128]{2,1,0:T(8,128)(4,1)S(1)} %iota_compare_fusion.7, bf16[9,16,32,128]{3,2,1,0:T(8,128)(2,1)} %get-tuple-element.147, s32[]{:T(128)S(6)} %copy.149), kind=kOutput, calls=%fused_computation.5.clone.1 | convolution fusion | flops 135262208 | bytes 4358148 | tf_op jit(solution)/shard_map/while/body/eval_jaxpr/mqd,mkpd->mqkp/dot_general | solution.py:24
  134.2 7.4 %all-to-all-start.2 = ((f32[16,9,8]{1,2,0:T(8,128)}), f32[16,9,8]{1,2,0:T(8,128)S(1)}, u32[]{:S(2)}, u32[]{:S(2)}) async-start(f32[16,9,8]{1,2,0:T(8,128)} %copy.121), calls=%async_computation.2 | async-start | bytes 131072 | tf_op jit(solution)/shard_map/all_to_all | solution.py:132
  141.6 6.9 %all-to-all-done.2 = f32[16,9,8]{1,2,0:T(8,128)S(1)} async-done(((f32[16,9,8]{1,2,0:T(8,128)}), f32[16,9,8]{1,2,0:T(8,128)S(1)}, u32[]{:S(2)}, u32[]{:S(2)}) %all-to-all-start.2) | async-done | bytes 4640 | tf_op jit(solution)/shard_map/all_to_all | solution.py:132
  148.7 4.5 %gather_fusion.3 = f32[768]{0:T(1024)S(1)} fusion(f32[1152]{0:T(1024)S(1)} %reshape.259, s32[1024]{0:T(1024)S(1)} %pad_clamp_fusion.1), kind=kCustom, calls=%fused_computation.3 | custom fusion | bytes 9216 | tf_op jit(solution)/shard_map/jit(_take)/gather | solution.py:136
  (170 shorter events, 45.4 us)
Async XLA Ops:
  0.0 1.7 %copy-start = (s32[512]{0:T(512)S(1)}, s32[512]{0:T(512)}, u32[]{:S(2)}) copy-start(s32[512]{0:T(512)} %param.13) | copy-start | bytes 6148
  1.7 16.9 %copy-start.3 = (bf16[32,32,128]{2,1,0:T(8,128)(2,1)S(1)}, bf16[32,32,128]{2,1,0:T(8,128)(2,1)}, u32[]{:S(2)}) copy-start(bf16[32,32,128]{2,1,0:T(8,128)(2,1)} %param.10) | copy-start | bytes 786436
  11.2 14.0 %all-to-all-start = ((bf16[16,9,8]{1,2,0:T(8,128)(2,1)}), bf16[16,9,8]{1,2,0:T(8,128)(2,1)S(1)}, u32[]{:S(2)}, u32[]{:S(2)}) async-start(bf16[16,9,8]{1,2,0:T(8,128)(2,1)} %copy.114), calls=%async_computation | async-start | bytes 65536 | tf_op jit(solution)/shard_map/all_to_all | solution.py:122
  25.2 29.5 %all-to-all-start.1 = ((bf16[16,9,32,128]{3,2,1,0:T(8,128)(2,1)}), bf16[16,9,32,128]{3,2,1,0:T(8,128)(2,1)}, u32[]{:S(2)}, u32[]{:S(2)}) async-start(bf16[16,9,32,128]{3,2,1,0:T(8,128)(2,1)} %copy.118), calls=%async_computation.1 | async-start | bytes 2359296 | tf_op jit(solution)/shard_map/all_to_all | solution.py:121
  30.0 5.5 %copy-start.4 = (f32[4]{0:T(128)S(1)}, f32[4]{0:T(128)}, u32[]{:S(2)}) copy-start(f32[4]{0:T(128)} %param.17) | copy-start | bytes 52
  30.0 6.2 %copy-start.2 = (s32[32,128,128]{2,1,0:T(8,128)S(1)}, s32[32,128,128]{2,1,0:T(8,128)}, u32[]{:S(2)}) copy-start(s32[32,128,128]{2,1,0:T(8,128)} %param.15) | copy-start | bytes 6291460
  41.0 13.7 %copy-start.1 = (s32[32]{0:T(128)S(1)}, s32[32]{0:T(128)}, u32[]{:S(2)}) copy-start(s32[32]{0:T(128)} %param.16) | copy-start | bytes 388
  134.2 14.3 %all-to-all-start.2 = ((f32[16,9,8]{1,2,0:T(8,128)}), f32[16,9,8]{1,2,0:T(8,128)S(1)}, u32[]{:S(2)}, u32[]{:S(2)}) async-start(f32[16,9,8]{1,2,0:T(8,128)} %copy.121), calls=%async_computation.2 | async-start | bytes 131072 | tf_op jit(solution)/shard_map/all_to_all | solution.py:132
  148.7 4.6 %copy-start.5 = (s32[32]{0:T(128)S(1)}, s32[32]{0:T(128)}, u32[]{:S(2)}) copy-start(s32[32]{0:T(128)} %param.12) | copy-start | bytes 388
where the time goes:
time: 155 us; the launch traced here: 154 us
  local copies, waits for them, and re-layouts  62 us (40%)
  matrix products  35.5 us (23%)
  waiting for transfers between devices  20.4 us (13%)
  starting transfers between devices  19.2 us (12%)
  other arithmetic  16 us (10%)
    gather x27, local copies, waits for them, and re-layouts, one_block(): return score_block(query_part, decoded[row_part], lengths[row_part])  38.8 us
    dot_general x9, matrix products, score_block(): jnp.einsum('mqd,mkpd->mqkp', query_rows, token_rows, preferred_element_ty...  35 us
    all_to_all x1, waiting for transfers between devices, local(): lax.all_to_all(outgoing, 'shard', split_axis=0, concat_axis=0, tiled=True)  8.68 us
    all_to_all x1, starting transfers between devices, local(): lax.all_to_all(visited, 'shard', split_axis=0, concat_axis=0, tiled=True)  7.39 us
    all_to_all x1, starting transfers between devices, local(): lax.all_to_all(target.astype(jnp.bfloat16), 'shard', split_axis=0, concat...  7.39 us
    all_to_all x1, waiting for transfers between devices, local(): lax.all_to_all(visited, 'shard', split_axis=0, concat_axis=0, tiled=True)  6.88 us
    gather x5, local copies, waits for them, and re-layouts, local(): jnp.take_along_axis(slot_of, jnp.clip(holders, 0, device_count - 1), axis=1)  5.46 us
    gather x5, local copies, waits for them, and re-layouts, local(): stored = placement_map[candidates]  5.3 us
  transfers between devices with their start and end apart: 3, of which 3 were waited for; matrix products, arithmetic and copies ran while one was open for 12% of the time, Pallas kernels for 0%

commit v1 on v0

v1 whole, which is shorter than its diff:
```python
import functools

import jax
import jax.numpy as jnp
from jax import lax
from jax.experimental import pallas as pl
from jax.experimental.pallas import tpu as pltpu
from jax.sharding import PartitionSpec as P

OWNERS_Q = 3
CHUNK = 8
LANES = 128
EPSILON = 1e-06
AXIS = "shard"

NT = (((1,), (1,)), ((), ()))
NN = (((1,), (0,)), ((), ()))


def dot(a, b, dims):
    return lax.dot_general(a, b, dims, preferred_element_type=jnp.float32)


def split_dot(a, b, dims, exact_left):
    full = b if exact_left else a
    high = full.astype(jnp.bfloat16)
    low = (full - high.astype(jnp.float32)).astype(jnp.bfloat16)
    if exact_left:
        return dot(a, high, dims) + dot(a, low, dims)
    return dot(high, b, dims) + dot(low, b, dims)


def iota(shape, axis):
    return lax.broadcasted_iota(jnp.int32, shape, axis)


def kernel(
    n,
    cap,
    weights_ref,
    lengths_ref,
    queries_ref,
    candidates_ref,
    count_ref,
    placement_ref,
    base_hbm,
    codes_hbm,
    out_ref,
    base_ref,
    codes_ref,
    tokens_ref,
    send_ref,
    recv_ref,
    source_vmem,
    source_smem,
    maxima_ref,
    scores_ref,
    returned_ref,
    load_sem,
    source_sem,
    send_sem,
    recv_sem,
    back_send_sem,
    back_recv_sem,
):
    me = lax.axis_index(AXIS)
    rows, plen, dim = base_ref.shape
    count, qlen, _ = queries_ref.shape
    slots = candidates_ref.shape[1]
    total = placement_ref.shape[1]
    padded = scores_ref.shape[1]
    per_group = LANES // rows
    groups = n // per_group
    steps = n * cap // CHUNK

    def partner(offset):
        return lax.rem(me + offset, n)

    def holder_of_mine(offset):
        return lax.rem(me + n - offset, n)

    load_base = pltpu.make_async_copy(base_hbm, base_ref, load_sem.at[0])
    load_codes = pltpu.make_async_copy(codes_hbm, codes_ref, load_sem.at[1])
    load_base.start()
    load_codes.start()

    barrier = pltpu.get_barrier_semaphore()

    def greet(offset, carry):
        pl.semaphore_signal(barrier, inc=1, device_id={AXIS: partner(offset)}, device_id_type=pl.DeviceIdType.MESH)
        return carry

    lax.fori_loop(1, n, greet, 0)

    candidates = candidates_ref[...]
    counted = count_ref[...]
    placement = placement_ref[...].astype(jnp.float32)
    passage_iota = iota((count, total), 1)
    slot_iota = iota((count, slots), 1)
    holder_iota = iota((count, LANES), 1)
    stored_cols = []
    present = jnp.zeros((count, LANES), jnp.float32)
    for c in range(slots):
        hit = passage_iota == candidates[:, c : c + 1]
        found = jnp.sum(jnp.where(hit, placement, 0.0), axis=1, keepdims=True).astype(jnp.int32)
        stored_cols.append(found)
        holder = jnp.where(c < counted, found // rows, -1)
        present = jnp.where(holder_iota == holder, 1.0, present)
    earlier = (iota((count, count), 1) < iota((count, count), 0)).astype(jnp.bfloat16)
    slot_of = dot(earlier, present.astype(jnp.bfloat16), NN)
    slot_of = jnp.where(present > 0.0, slot_of, -1.0).astype(jnp.bfloat16)
    eye = (iota((n, LANES), 0) == iota((n, LANES), 1)).astype(jnp.bfloat16)
    slot_by_holder = dot(eye, slot_of, NT)
    query_iota = iota((n, count), 1)
    lane_iota = iota((n, LANES), 1)
    source = jnp.zeros((n, LANES), jnp.int32)
    for s in range(cap):
        which = jnp.sum(
            jnp.where(slot_by_holder == float(s), query_iota.astype(jnp.float32), 0.0), axis=1, keepdims=True
        ).astype(jnp.int32)
        source = jnp.where(lane_iota == s, which, source)
    source_vmem[...] = source

    maxima_ref[...] = jnp.zeros_like(maxima_ref)
    scores_ref[...] = jnp.zeros_like(scores_ref)

    to_scalar = pltpu.make_async_copy(source_vmem, source_smem, source_sem)
    to_scalar.start()
    to_scalar.wait()

    def query_for(holder, s):
        return queries_ref[jnp.minimum(jnp.maximum(source_smem[holder, s], 0), count - 1)]

    def pack(offset, carry):
        holder = partner(offset)
        for s in range(cap):
            send_ref[offset, s] = query_for(holder, s)
        return carry

    def outgoing(offset):
        return pltpu.make_async_remote_copy(
            src_ref=send_ref.at[offset],
            dst_ref=recv_ref.at[offset],
            send_sem=send_sem.at[offset],
            recv_sem=recv_sem.at[offset],
            device_id={AXIS: partner(offset)},
            device_id_type=pl.DeviceIdType.MESH,
        )

    pack(1, 0)
    pl.semaphore_wait(barrier, n - 1)

    def pack_and_send(offset, carry):
        pack(offset + 1, 0)
        outgoing(offset).start()
        return carry

    lax.fori_loop(1, n - 1, pack_and_send, 0)
    for s in range(cap):
        recv_ref[0, s] = query_for(me, s)
    outgoing(n - 1).start()

    load_base.wait()
    load_codes.wait()
    token_iota = iota((plen, dim), 0)

    def decode(r, carry):
        codes = codes_ref[r]
        low = jnp.where(codes < 1, weights_ref[0, 0], weights_ref[0, 1])
        high = jnp.where(codes < 3, weights_ref[0, 2], weights_ref[0, 3])
        summed = base_ref[r].astype(jnp.float32) + jnp.where(codes < 2, low, high)
        inverse = lax.rsqrt(jnp.sum(summed * summed, axis=1, keepdims=True) + EPSILON)
        unit = summed * inverse
        unit = jnp.where(token_iota < lengths_ref[0, r], unit, unit[0:1, :])
        tokens_ref[r] = unit.astype(jnp.bfloat16)
        return carry

    lax.fori_loop(0, rows, decode, 0)

    row_start = lax.rem(me, per_group) * rows
    gather_tokens = (iota((CHUNK, CHUNK * qlen), 1) // qlen == iota((CHUNK, CHUNK * qlen), 0)).astype(jnp.bfloat16)

    def back(offset):
        return pltpu.make_async_remote_copy(
            src_ref=scores_ref.at[offset],
            dst_ref=returned_ref.at[me],
            send_sem=back_send_sem.at[offset],
            recv_sem=back_recv_sem.at[me],
            device_id={AXIS: holder_of_mine(offset)},
            device_id_type=pl.DeviceIdType.MESH,
        )

    def send_back(offset, carry):
        back(offset).start()
        return carry

    def chunk(i, carry):
        first, last = i * CHUNK, i * CHUNK + CHUNK - 1
        lax.fori_loop((first - 1 + cap) // cap, last // cap + 1, wait_query_if, 0)
        parts = [recv_ref[(first + g) // cap, lax.rem(first + g, cap)] for g in range(CHUNK)]
        block = jnp.concatenate(parts, axis=0)

        def one_row(r, inner):
            similar = dot(tokens_ref[r], block, NT)
            maxima_ref[pl.ds(row_start + r, 1), :] = jnp.max(similar, axis=0, keepdims=True)
            return inner

        lax.fori_loop(0, rows, one_row, 0, unroll=4)
        scored = split_dot(gather_tokens, maxima_ref[...], NT, True)
        for g in range(CHUNK):
            scores_ref[(first + g) // cap, pl.ds(lax.rem(first + g, cap), 1), :] = scored[g : g + 1, :]
        lax.fori_loop(jnp.maximum(done_before(i - 1), 1), jnp.maximum(done_before(i), 1), send_back, 0)
        return carry

    def done_before(i):
        return jnp.maximum(i, 0) * CHUNK // cap

    def wait_query_if(offset, carry):
        @pl.when(offset >= 1)
        def _():
            outgoing(offset).wait_recv()

        return carry

    lax.fori_loop(0, steps, chunk, 0)

    def wait_sent(offset, carry):
        outgoing(offset).wait_send()
        return carry

    lax.fori_loop(1, n, wait_sent, 0)
    lax.fori_loop(max((steps - 1) * CHUNK // cap, 1), n, send_back, 0)
    returned_ref[me] = scores_ref[0]

    spread = (iota((LANES, n * padded), 1) // padded == iota((LANES, n * padded), 0)).astype(jnp.bfloat16)
    wide_slot = dot(slot_of, spread, NN)
    wide_iota = iota((count, n * padded), 1)
    chosen = wide_slot == lax.rem(wide_iota, padded).astype(jnp.float32)
    picks = jnp.concatenate(
        [
            jnp.where(chosen & (wide_iota // (padded * per_group) == g), 1.0, 0.0).astype(jnp.bfloat16)
            for g in range(groups)
        ],
        axis=0,
    )

    def wait_back(offset, carry):
        peer = partner(offset)
        pltpu.make_async_remote_copy(
            src_ref=scores_ref.at[offset],
            dst_ref=returned_ref.at[peer],
            send_sem=back_send_sem.at[offset],
            recv_sem=back_recv_sem.at[peer],
            device_id={AXIS: peer},
            device_id_type=pl.DeviceIdType.MESH,
        ).wait_recv()
        return carry

    lax.fori_loop(1, n, wait_back, 0)
    values = split_dot(picks, returned_ref[...].reshape(n * padded, LANES), NN, True)
    result = jnp.zeros((count, slots), jnp.float32)
    for c in range(slots):
        kept = jnp.zeros((count, LANES), jnp.float32)
        for g in range(groups):
            kept = jnp.where(
                holder_iota + g * LANES == stored_cols[c], values[g * count : (g + 1) * count, :], kept
            )
        result = jnp.where(slot_iota == c, jnp.sum(kept, axis=1, keepdims=True), result)
    out_ref[...] = jnp.where(slot_iota < counted, result, 0.0)

    def wait_back_sent(offset, carry):
        back(offset).wait_send()
        return carry

    lax.fori_loop(1, n, wait_back_sent, 0)


def local(
    query_tokens,
    candidates,
    cand_count,
    placement_map,
    passage_base,
    residual_codes,
    passage_lengths,
    bucket_weights,
):
    n = lax.axis_size(AXIS)
    count, qlen, dim = query_tokens.shape
    slots = candidates.shape[1]
    rows, plen, _ = passage_base.shape
    cap = count * OWNERS_Q // n + 3
    padded = -(-cap // 8) * 8
    vmem = pl.BlockSpec(memory_space=pltpu.VMEM)
    smem = pl.BlockSpec(memory_space=pltpu.SMEM)
    anywhere = pl.BlockSpec(memory_space=pl.ANY)
    return pl.pallas_call(
        functools.partial(kernel, n, cap),
        out_shape=jax.ShapeDtypeStruct((count, slots), jnp.float32),
        in_specs=[smem, smem, vmem, vmem, vmem, vmem, anywhere, anywhere],
        out_specs=vmem,
        scratch_shapes=[
            pltpu.VMEM((rows, plen, dim), passage_base.dtype),
            pltpu.VMEM((rows, plen, dim), jnp.int32),
            pltpu.VMEM((rows, plen, dim), jnp.bfloat16),
            pltpu.VMEM((n, cap, qlen, dim), jnp.bfloat16),
            pltpu.VMEM((n, cap, qlen, dim), jnp.bfloat16),
            pltpu.VMEM((n, LANES), jnp.int32),
            pltpu.SMEM((n, LANES), jnp.int32),
            pltpu.VMEM((LANES, CHUNK * qlen), jnp.float32),
            pltpu.VMEM((n, padded, LANES), jnp.float32),
            pltpu.VMEM((n, padded, LANES), jnp.float32),
            pltpu.SemaphoreType.DMA((2,)),
            pltpu.SemaphoreType.DMA,
            pltpu.SemaphoreType.DMA((n,)),
            pltpu.SemaphoreType.DMA((n,)),
            pltpu.SemaphoreType.DMA((n,)),
            pltpu.SemaphoreType.DMA((n,)),
        ],
        compiler_params=pltpu.CompilerParams(
            collective_id=0, has_side_effects=True, vmem_limit_bytes=48 * 1024 * 1024
        ),
        name="rerank",
    )(
        bucket_weights.reshape(1, -1),
        passage_lengths.reshape(1, -1),
        query_tokens,
        candidates,
        cand_count.reshape(-1, 1),
        placement_map.reshape(1, -1),
        passage_base,
        residual_codes,
    )


def solution(mesh):
    split = P(("groups", "shard"))
    return jax.shard_map(
        local,
        mesh=mesh,
        in_specs=(
            P(("groups", "shard"), None, None),
            P(("groups", "shard"), None),
            split,
            P("groups"),
            P(("groups", "shard"), None, None),
            P(("groups", "shard"), None, None),
            split,
            P("groups"),
        ),
        out_specs=P(("groups", "shard"), None),
        check_vma=False,
    )
```

time: 155 us -> 69 us (0.45)
  Pallas kernels: 0 us -> 60.7 us
  local copies, waits for them, and re-layouts: 62 us -> 7.94 us
  matrix products: 35.5 us -> 0 us
  waiting for transfers between devices: 20.4 us -> 0 us
  starting transfers between devices: 19.2 us -> 0 us
  other arithmetic: 16 us -> 0 us
    pallas_call x0 -> x1, Pallas kernels: none -> 60.7 us  [local(): pl.pallas_call(functools.partial(kernel, n, cap), out_shape=jax.ShapeDtyp...]
    gather x39 -> x0, local copies, waits for them, and re-layouts: 54.1 us -> none  [the longest x27 38.8 us: one_block(): return score_block(query_part, decoded[row_part], lengths[row_part])]
    dot_general x10 -> x0, matrix products: 35.5 us -> none  [the longest x9 35 us: score_block(): jnp.einsum('mqd,mkpd->mqkp', query_rows, token_rows, preferred_element_ty...]
    all_to_all x3 -> x0, waiting for transfers between devices: 20.4 us -> none  [the longest x1 8.68 us: local(): lax.all_to_all(outgoing, 'shard', split_axis=0, concat_axis=0, tiled=True)]
    all_to_all x3 -> x0, starting transfers between devices: 19.2 us -> none  [the longest x1 7.39 us: local(): lax.all_to_all(visited, 'shard', split_axis=0, concat_axis=0, tiled=True)]
    reduce_sum x13 -> x0, other arithmetic: 8.62 us -> none  [the longest x1 4.81 us: decode(): jnp.sum(summed * summed, axis=-1, keepdims=True) + epsilon]
    unnamed x12 -> x13, local copies, waits for them, and re-layouts: 0.04 us -> 6.53 us
    convert_element_type x4 -> x0, other arithmetic: 4.62 us -> none  [the longest x1 4.59 us: decode(): return (summed * inverse_norm).astype(jnp.bfloat16)]
  transfers between devices with their start and end apart: 3 -> 0, of which waited for: 3 -> 0; matrix products, arithmetic and copies ran while one was open for 12% -> 0% of each run, Pallas kernels for 0% -> 0%
where the time goes in v1:
time: 69 us; the launch traced here: 68.6 us
  Pallas kernels  60.7 us (88%)
  local copies, waits for them, and re-layouts  7.94 us (12%)
    pallas_call x1, Pallas kernels, local(): pl.pallas_call(functools.partial(kernel, n, cap), out_shape=jax.ShapeDtyp...  60.7 us
    unnamed x13, local copies, waits for them, and re-layouts  6.53 us

profile of v1, /device:TPU:0, one launch (start us, length us, event | category | flops | bytes accessed | tf_op | source)
XLA Modules:
  0.0 68.6 jit_solution(3114500879889091043)
XLA Ops:
  0.0 0.8 %copy.9.candidates_ref = s32[32,24]{1,0:T(8,128)S(1)} copy(s32[32,24]{0,1:T(8,128)} %param.9) | data formatting | bytes 6144 | tf_op args[1]
  0.8 0.7 %copy.10.count_ref = s32[32,1]{1,0:T(8,128)S(1)} copy(s32[32,1]{0,1:T(1,128)} %bitcast.7) | data formatting | bytes 256 | tf_op jit(solution)/shard_map/reshape | solution.py:329
  1.5 0.0 copy-start
  1.5 1.6 %copy-done = s32[32,128,128]{2,1,0:T(8,128)S(1)} copy-done((s32[32,128,128]{2,1,0:T(8,128)S(1)}, s32[32,128,128]{2,1,0:T(8,128)}, u32[]{:S(2)}) %copy-start) | copy-done | bytes 2097176
  3.1 0.0 copy-start.1
  3.1 1.2 %copy-done.1 = bf16[32,128,128]{2,1,0:T(8,128)(2,1)S(1)} copy-done((bf16[32,128,128]{2,1,0:T(8,128)(2,1)S(1)}, bf16[32,128,128]{2,1,0:T(8,128)(2,1)}, u32[]{:S(2)}) %copy-start.1) | copy-done | bytes 1048600
  4.3 0.0 copy-start.2
  4.3 0.9 %copy-done.2 = bf16[32,32,128]{2,1,0:T(8,128)(2,1)S(1)} copy-done((bf16[32,32,128]{2,1,0:T(8,128)(2,1)S(1)}, bf16[32,32,128]{2,1,0:T(8,128)(2,1)}, u32[]{:S(2)}) %copy-start.2) | copy-done | bytes 262168
  5.3 0.0 copy-start.3
  5.3 0.7 copy-done.3
  6.0 0.0 copy-start.4
  6.0 0.7 copy-done.4
  6.6 0.0 copy-start.5
  6.6 0.7 copy-done.5
  7.3 60.7 %rerank.1 = f32[32,24]{1,0:T(8,128)S(1)} custom-call(f32[1,4]{1,0:T(1,128)S(1)} %bitcast.5, s32[1,32]{1,0:T(1,128)S(1)} %bitcast.6, bf16[32,32,128]{2,1,0:T(8,128)(2,1)S(1)} %copy-done.2, s32[32,24]{1,0:T(8,128)S(1)} %copy.9.candidates_ref, s32[32,1]{1,0:T(8,128)S(1)} %copy.10.count_ref, s32[1,512]{1,0:T(1,128)S(1)} %bitcast.4, ...), custom_call_target="tpu_custom_call" | custom-call | tf_op jit(solution)/shard_map/rerank/pallas_call | solution.py:297
  68.0 0.7 copy.11
Async XLA Ops:
  1.5 1.6 %copy-start = (s32[32,128,128]{2,1,0:T(8,128)S(1)}, s32[32,128,128]{2,1,0:T(8,128)}, u32[]{:S(2)}) copy-start(s32[32,128,128]{2,1,0:T(8,128)} %codes_hbm.1) | copy-start | bytes 6291460
  3.1 1.2 %copy-start.1 = (bf16[32,128,128]{2,1,0:T(8,128)(2,1)S(1)}, bf16[32,128,128]{2,1,0:T(8,128)(2,1)}, u32[]{:S(2)}) copy-start(bf16[32,128,128]{2,1,0:T(8,128)(2,1)} %base_hbm.1) | copy-start | bytes 3145732
  4.3 0.9 %copy-start.2 = (bf16[32,32,128]{2,1,0:T(8,128)(2,1)S(1)}, bf16[32,32,128]{2,1,0:T(8,128)(2,1)}, u32[]{:S(2)}) copy-start(bf16[32,32,128]{2,1,0:T(8,128)(2,1)} %queries_ref.1) | copy-start | bytes 786436
  5.3 0.7 copy-start.3
  6.0 0.7 copy-start.4
  6.6 0.7 copy-start.5

commit v2 on v1

--- a/solution.py
+++ b/solution.py
@@ -37,15 +37,21 @@
 def kernel(
     n,
     cap,
+    weights_hbm,
+    lengths_hbm,
+    queries_hbm,
+    candidates_hbm,
+    count_hbm,
+    placement_hbm,
+    base_hbm,
+    codes_hbm,
+    out_ref,
     weights_ref,
     lengths_ref,
     queries_ref,
     candidates_ref,
     count_ref,
     placement_ref,
-    base_hbm,
-    codes_hbm,
-    out_ref,
     base_ref,
     codes_ref,
     tokens_ref,
@@ -66,7 +72,7 @@
     me = lax.axis_index(AXIS)
     rows, plen, dim = base_ref.shape
     count, qlen, _ = queries_ref.shape
-    slots = candidates_ref.shape[1]
+    slots = candidates_ref.shape[0]
     total = placement_ref.shape[1]
     padded = scores_ref.shape[1]
     per_group = LANES // rows
@@ -79,10 +85,19 @@
     def holder_of_mine(offset):
         return lax.rem(me + n - offset, n)
 
-    load_base = pltpu.make_async_copy(base_hbm, base_ref, load_sem.at[0])
-    load_codes = pltpu.make_async_copy(codes_hbm, codes_ref, load_sem.at[1])
-    load_base.start()
-    load_codes.start()
+    pairs = (
+        (candidates_hbm, candidates_ref),
+        (count_hbm, count_ref),
+        (placement_hbm, placement_ref),
+        (queries_hbm, queries_ref),
+        (weights_hbm, weights_ref),
+        (lengths_hbm, lengths_ref),
+        (base_hbm, base_ref),
+        (codes_hbm, codes_ref),
+    )
+    loads = [pltpu.make_async_copy(src, dst, load_sem.at[i]) for i, (src, dst) in enumerate(pairs)]
+    for load in loads:
+        load.start()
 
     barrier = pltpu.get_barrier_semaphore()
 
@@ -92,8 +107,16 @@
 
     lax.fori_loop(1, n, greet, 0)
 
-    candidates = candidates_ref[...]
-    counted = count_ref[...]
+    for load in loads[:3]:
+        load.wait()
+    square = (iota((count, count), 0) == iota((count, count), 1)).astype(jnp.bfloat16)
+
+    def upright(flat):
+        return dot(square, flat.astype(jnp.float32).astype(jnp.bfloat16), NT).astype(jnp.int32)
+
+    listed = candidates_ref[...]
+    candidates = upright(lax.div(listed, 64)) * 64 + upright(lax.rem(listed, 64))
+    counted = upright(jnp.broadcast_to(count_ref[...], (8, count)))[:, 0:1]
     placement = placement_ref[...].astype(jnp.float32)
     passage_iota = iota((count, total), 1)
     slot_iota = iota((count, slots), 1)
@@ -104,7 +127,7 @@
         hit = passage_iota == candidates[:, c : c + 1]
         found = jnp.sum(jnp.where(hit, placement, 0.0), axis=1, keepdims=True).astype(jnp.int32)
         stored_cols.append(found)
-        holder = jnp.where(c < counted, found // rows, -1)
+        holder = jnp.where(c < counted, lax.div(found, rows), -1)
         present = jnp.where(holder_iota == holder, 1.0, present)
     earlier = (iota((count, count), 1) < iota((count, count), 0)).astype(jnp.bfloat16)
     slot_of = dot(earlier, present.astype(jnp.bfloat16), NN)
@@ -126,6 +149,7 @@
 
     to_scalar = pltpu.make_async_copy(source_vmem, source_smem, source_sem)
     to_scalar.start()
+    loads[3].wait()
     to_scalar.wait()
 
     def query_for(holder, s):
@@ -134,13 +158,13 @@
     def pack(offset, carry):
         holder = partner(offset)
         for s in range(cap):
-            send_ref[offset, s] = query_for(holder, s)
+            send_ref[offset * cap + s] = query_for(holder, s)
         return carry
 
     def outgoing(offset):
         return pltpu.make_async_remote_copy(
-            src_ref=send_ref.at[offset],
-            dst_ref=recv_ref.at[offset],
+            src_ref=send_ref.at[pl.ds(offset * cap, cap)],
+            dst_ref=recv_ref.at[pl.ds(offset * cap, cap)],
             send_sem=send_sem.at[offset],
             recv_sem=recv_sem.at[offset],
             device_id={AXIS: partner(offset)},
@@ -157,11 +181,11 @@
 
     lax.fori_loop(1, n - 1, pack_and_send, 0)
     for s in range(cap):
-        recv_ref[0, s] = query_for(me, s)
+        recv_ref[s] = query_for(me, s)
     outgoing(n - 1).start()
 
-    load_base.wait()
-    load_codes.wait()
+    for load in loads[4:]:
+        load.wait()
     token_iota = iota((plen, dim), 0)
 
     def decode(r, carry):
@@ -177,8 +201,7 @@
 
     lax.fori_loop(0, rows, decode, 0)
 
-    row_start = lax.rem(me, per_group) * rows
-    gather_tokens = (iota((CHUNK, CHUNK * qlen), 1) // qlen == iota((CHUNK, CHUNK * qlen), 0)).astype(jnp.bfloat16)
+    gather_tokens = (lax.div(iota((CHUNK, CHUNK * qlen), 1), qlen) == iota((CHUNK, CHUNK * qlen), 0)).astype(jnp.bfloat16)
 
     def back(offset):
         return pltpu.make_async_remote_copy(
@@ -194,26 +217,25 @@
         back(offset).start()
         return carry
 
-    def chunk(i, carry):
-        first, last = i * CHUNK, i * CHUNK + CHUNK - 1
-        lax.fori_loop((first - 1 + cap) // cap, last // cap + 1, wait_query_if, 0)
-        parts = [recv_ref[(first + g) // cap, lax.rem(first + g, cap)] for g in range(CHUNK)]
-        block = jnp.concatenate(parts, axis=0)
-
-        def one_row(r, inner):
-            similar = dot(tokens_ref[r], block, NT)
-            maxima_ref[pl.ds(row_start + r, 1), :] = jnp.max(similar, axis=0, keepdims=True)
-            return inner
-
-        lax.fori_loop(0, rows, one_row, 0, unroll=4)
+    def add_up(i):
         scored = split_dot(gather_tokens, maxima_ref[...], NT, True)
         for g in range(CHUNK):
-            scores_ref[(first + g) // cap, pl.ds(lax.rem(first + g, cap), 1), :] = scored[g : g + 1, :]
-        lax.fori_loop(jnp.maximum(done_before(i - 1), 1), jnp.maximum(done_before(i), 1), send_back, 0)
+            at = i * CHUNK + g
+            scores_ref[lax.div(at, cap), pl.ds(lax.rem(at, cap), 1), pl.ds(0, rows)] = scored[g : g + 1, :]
+
+    def chunk(i, carry):
+        first = i * CHUNK
+        lax.fori_loop(lax.div(first - 1 + cap, cap), lax.div(first + CHUNK - 1, cap) + 1, wait_query_if, 0)
+        lax.fori_loop(jnp.maximum(done_before(i - 2), 1), jnp.maximum(done_before(i - 1), 1), send_back, 0)
+        add_up(jnp.maximum(i - 1, 0))
+        block = recv_ref[pl.ds(first, CHUNK)].reshape(CHUNK * qlen, dim)
+        for r in range(rows):
+            similar = dot(tokens_ref[r], block, NT)
+            maxima_ref[r : r + 1, :] = jnp.max(similar, axis=0, keepdims=True)
         return carry
 
     def done_before(i):
-        return jnp.maximum(i, 0) * CHUNK // cap
+        return lax.div(jnp.maximum(i, 0) * CHUNK, cap)
 
     def wait_query_if(offset, carry):
         @pl.when(offset >= 1)
@@ -223,22 +245,23 @@
         return carry
 
     lax.fori_loop(0, steps, chunk, 0)
+    add_up(steps - 1)
 
     def wait_sent(offset, carry):
         outgoing(offset).wait_send()
         return carry
 
     lax.fori_loop(1, n, wait_sent, 0)
-    lax.fori_loop(max((steps - 1) * CHUNK // cap, 1), n, send_back, 0)
+    lax.fori_loop(max((steps - 2) * CHUNK // cap, 1), n, send_back, 0)
     returned_ref[me] = scores_ref[0]
 
-    spread = (iota((LANES, n * padded), 1) // padded == iota((LANES, n * padded), 0)).astype(jnp.bfloat16)
+    spread = (lax.div(iota((LANES, n * padded), 1), padded) == iota((LANES, n * padded), 0)).astype(jnp.bfloat16)
     wide_slot = dot(slot_of, spread, NN)
     wide_iota = iota((count, n * padded), 1)
     chosen = wide_slot == lax.rem(wide_iota, padded).astype(jnp.float32)
     picks = jnp.concatenate(
         [
-            jnp.where(chosen & (wide_iota // (padded * per_group) == g), 1.0, 0.0).astype(jnp.bfloat16)
+            jnp.where(chosen & (lax.div(wide_iota, padded * per_group) == g), 1.0, 0.0).astype(jnp.bfloat16)
             for g in range(groups)
         ],
         axis=0,
@@ -257,7 +280,8 @@
         return carry
 
     lax.fori_loop(1, n, wait_back, 0)
-    values = split_dot(picks, returned_ref[...].reshape(n * padded, LANES), NN, True)
+    placed = [pltpu.roll(returned_ref[k], k % per_group * rows, 1) for k in range(n)]
+    values = split_dot(picks, jnp.concatenate(placed, axis=0), NN, True)
     result = jnp.zeros((count, slots), jnp.float32)
     for c in range(slots):
         kept = jnp.zeros((count, LANES), jnp.float32)
@@ -291,26 +315,32 @@
     rows, plen, _ = passage_base.shape
     cap = count * OWNERS_Q // n + 3
     padded = -(-cap // 8) * 8
+    total = placement_map.shape[0]
     vmem = pl.BlockSpec(memory_space=pltpu.VMEM)
-    smem = pl.BlockSpec(memory_space=pltpu.SMEM)
-    anywhere = pl.BlockSpec(memory_space=pl.ANY)
+    hbm = pl.BlockSpec(memory_space=pltpu.HBM)
     return pl.pallas_call(
         functools.partial(kernel, n, cap),
         out_shape=jax.ShapeDtypeStruct((count, slots), jnp.float32),
-        in_specs=[smem, smem, vmem, vmem, vmem, vmem, anywhere, anywhere],
+        in_specs=[hbm] * 8,
         out_specs=vmem,
         scratch_shapes=[
+            pltpu.SMEM((1, bucket_weights.shape[0]), jnp.float32),
+            pltpu.SMEM((1, rows), jnp.int32),
+            pltpu.VMEM((count, qlen, dim), jnp.bfloat16),
+            pltpu.VMEM((slots, count), jnp.int32),
+            pltpu.VMEM((1, count), jnp.int32),
+            pltpu.VMEM((1, total), jnp.int32),
             pltpu.VMEM((rows, plen, dim), passage_base.dtype),
             pltpu.VMEM((rows, plen, dim), jnp.int32),
             pltpu.VMEM((rows, plen, dim), jnp.bfloat16),
-            pltpu.VMEM((n, cap, qlen, dim), jnp.bfloat16),
-            pltpu.VMEM((n, cap, qlen, dim), jnp.bfloat16),
+            pltpu.VMEM((n * cap, qlen, dim), jnp.bfloat16),
+            pltpu.VMEM((n * cap, qlen, dim), jnp.bfloat16),
             pltpu.VMEM((n, LANES), jnp.int32),
             pltpu.SMEM((n, LANES), jnp.int32),
-            pltpu.VMEM((LANES, CHUNK * qlen), jnp.float32),
+            pltpu.VMEM((rows, CHUNK * qlen), jnp.float32),
             pltpu.VMEM((n, padded, LANES), jnp.float32),
             pltpu.VMEM((n, padded, LANES), jnp.float32),
-            pltpu.SemaphoreType.DMA((2,)),
+            pltpu.SemaphoreType.DMA((8,)),
             pltpu.SemaphoreType.DMA,
             pltpu.SemaphoreType.DMA((n,)),
             pltpu.SemaphoreType.DMA((n,)),
@@ -318,15 +348,15 @@
             pltpu.SemaphoreType.DMA((n,)),
         ],
         compiler_params=pltpu.CompilerParams(
-            collective_id=0, has_side_effects=True, vmem_limit_bytes=48 * 1024 * 1024
+            collective_id=0, has_side_effects=True, vmem_limit_bytes=60 * 1024 * 1024
         ),
         name="rerank",
     )(
         bucket_weights.reshape(1, -1),
         passage_lengths.reshape(1, -1),
         query_tokens,
-        candidates,
-        cand_count.reshape(-1, 1),
+        candidates.T,
+        cand_count.reshape(1, -1),
         placement_map.reshape(1, -1),
         passage_base,
         residual_codes,

time: 69 us -> 47.8 us (0.69)
  Pallas kernels: 60.7 us -> 46.1 us
  local copies, waits for them, and re-layouts: 7.94 us -> 1.39 us
    pallas_call x1, Pallas kernels: 60.7 us -> 46.1 us  [local(): pl.pallas_call(functools.partial(kernel, n, cap), out_shape=jax.ShapeDtyp...]
    unnamed x13 -> x0, local copies, waits for them, and re-layouts: 6.53 us -> none
    reshape x1 -> x0, local copies, waits for them, and re-layouts: 0.74 us -> none  [local(): cand_count.reshape(-1, 1)]
    pallas_call x1, local copies, waits for them, and re-layouts: 0.67 us -> 1.39 us  [local(): pl.pallas_call(functools.partial(kernel, n, cap), out_shape=jax.ShapeDtyp...]
where the time goes in v2:
time: 47.8 us; the launch traced here: 47.5 us
  Pallas kernels  46.1 us (96%)
  local copies, waits for them, and re-layouts  1.39 us (3%)
    pallas_call x1, Pallas kernels, local(): pl.pallas_call(functools.partial(kernel, n, cap), out_shape=jax.ShapeDtyp...  46.1 us
    pallas_call x1, local copies, waits for them, and re-layouts, local(): pl.pallas_call(functools.partial(kernel, n, cap), out_shape=jax.ShapeDtyp...  1.39 us

profile of v2, /device:TPU:0, one launch (start us, length us, event | category | flops | bytes accessed | tf_op | source)
XLA Modules:
  0.0 47.5 jit_solution(14123436798995645913)
XLA Ops:
  0.0 46.1 %rerank.1 = f32[32,24]{1,0:T(8,128)} custom-call(f32[1,4]{1,0:T(1,128)} %bitcast.7, s32[1,32]{1,0:T(1,128)} %bitcast.8, bf16[32,32,128]{2,1,0:T(8,128)(2,1)} %queries_hbm.1, s32[24,32]{1,0:T(8,128)} %bitcast.5, s32[1,32]{1,0:T(1,128)} %bitcast.9, s32[1,512]{1,0:T(1,128)} %bitcast.6, bf16[32,128,128]{2,1,0:T(8,128)(2,1)} %base_hbm.1, s32[32,128,128]{2,1,0:T(8,128)} %codes_hbm.1), custom_call_target="tpu_custom_call" | custom-call | tf_op jit(solution)/shard_map/rerank/pallas_call | solution.py:321
  46.1 1.4 %copy.9 = f32[32,24]{0,1:T(8,128)} copy(f32[32,24]{1,0:T(8,128)} %rerank.1) | data formatting | bytes 6144 | tf_op jit(solution)/shard_map/rerank/pallas_call | solution.py:321

commit v3 on v2

--- a/solution.py
+++ b/solution.py
@@ -37,6 +37,8 @@
 def kernel(
     n,
     cap,
+    cold,
+    inner,
     weights_hbm,
     lengths_hbm,
     queries_hbm,
@@ -68,6 +70,12 @@
     recv_sem,
     back_send_sem,
     back_recv_sem,
+    line_send_sem,
+    line_recv_sem,
+    block_send_sem,
+    block_recv_sem,
+    late_send_sem,
+    late_recv_sem,
 ):
     me = lax.axis_index(AXIS)
     rows, plen, dim = base_ref.shape
@@ -77,13 +85,23 @@
     padded = scores_ref.shape[1]
     per_group = LANES // rows
     groups = n // per_group
+    hot = cap - cold
+    outer = n // inner
+    common = n * cold
+    common_steps = common // CHUNK
     steps = n * cap // CHUNK
-
-    def partner(offset):
-        return lax.rem(me + offset, n)
-
-    def holder_of_mine(offset):
-        return lax.rem(me + n - offset, n)
+    early_steps = common_steps * 2 // 3
+    my_outer, my_inner = lax.div(me, inner), lax.rem(me, inner)
+    tile = padded // 2
+
+    def shift(position):
+        return jnp.where(position == 0, 0, lax.rem(position + n // 2 - 2 + n - 1, n - 1) + 1)
+
+    def partner(position):
+        return lax.rem(me + shift(position), n)
+
+    def holder_of_mine(position):
+        return lax.rem(me + n - shift(position), n)
 
     pairs = (
         (candidates_hbm, candidates_ref),
@@ -138,10 +156,11 @@
     lane_iota = iota((n, LANES), 1)
     source = jnp.zeros((n, LANES), jnp.int32)
     for s in range(cap):
-        which = jnp.sum(
-            jnp.where(slot_by_holder == float(s), query_iota.astype(jnp.float32), 0.0), axis=1, keepdims=True
-        ).astype(jnp.int32)
-        source = jnp.where(lane_iota == s, which, source)
+        match = jnp.where(slot_by_holder == float(s), query_iota.astype(jnp.float32), 0.0)
+        which = jnp.sum(match, axis=1, keepdims=True)
+        if s >= cold:
+            which = jnp.broadcast_to(jnp.sum(which, axis=0, keepdims=True), which.shape)
+        source = jnp.where(lane_iota == s, which.astype(jnp.int32), source)
     source_vmem[...] = source
 
     maxima_ref[...] = jnp.zeros_like(maxima_ref)
@@ -155,34 +174,77 @@
     def query_for(holder, s):
         return queries_ref[jnp.minimum(jnp.maximum(source_smem[holder, s], 0), count - 1)]
 
-    def pack(offset, carry):
-        holder = partner(offset)
-        for s in range(cap):
-            send_ref[offset * cap + s] = query_for(holder, s)
-        return carry
-
-    def outgoing(offset):
+    def pack(position, carry):
+        holder = partner(position)
+        for s in range(cold):
+            send_ref[position * cold + s] = query_for(holder, s)
+        return carry
+
+    def outgoing(position):
         return pltpu.make_async_remote_copy(
-            src_ref=send_ref.at[pl.ds(offset * cap, cap)],
-            dst_ref=recv_ref.at[pl.ds(offset * cap, cap)],
-            send_sem=send_sem.at[offset],
-            recv_sem=recv_sem.at[offset],
-            device_id={AXIS: partner(offset)},
+            src_ref=send_ref.at[pl.ds(position * cold, cold)],
+            dst_ref=recv_ref.at[pl.ds(position * cold, cold)],
+            send_sem=send_sem.at[position],
+            recv_sem=recv_sem.at[position],
+            device_id={AXIS: partner(position)},
             device_id_type=pl.DeviceIdType.MESH,
         )
 
+    def along_line(place, slot):
+        rows_of = pl.ds(common + (my_inner * outer + slot) * hot, hot)
+        return pltpu.make_async_remote_copy(
+            src_ref=recv_ref.at[rows_of],
+            dst_ref=recv_ref.at[rows_of],
+            send_sem=line_send_sem.at[place],
+            recv_sem=line_recv_sem.at[slot],
+            device_id={AXIS: place * inner + my_inner},
+            device_id_type=pl.DeviceIdType.MESH,
+        )
+
+    def inside_block(place, slot):
+        rows_of = pl.ds(common + slot * outer * hot, outer * hot)
+        return pltpu.make_async_remote_copy(
+            src_ref=recv_ref.at[rows_of],
+            dst_ref=recv_ref.at[rows_of],
+            send_sem=block_send_sem.at[place],
+            recv_sem=block_recv_sem.at[slot],
+            device_id={AXIS: my_outer * inner + place},
+            device_id_type=pl.DeviceIdType.MESH,
+        )
+
+    for s in range(hot):
+        recv_ref[common + (my_inner * outer + my_outer) * hot + s] = query_for(me, cold + s)
     pack(1, 0)
     pl.semaphore_wait(barrier, n - 1)
 
-    def pack_and_send(offset, carry):
-        pack(offset + 1, 0)
-        outgoing(offset).start()
+    def start_line(k, carry):
+        along_line(lax.rem(my_outer + k, outer), my_outer).start()
+        return carry
+
+    lax.fori_loop(1, outer, start_line, 0)
+
+    def pack_and_send(position, carry):
+        pack(position + 1, 0)
+        outgoing(position).start()
         return carry
 
     lax.fori_loop(1, n - 1, pack_and_send, 0)
-    for s in range(cap):
+    for s in range(cold):
         recv_ref[s] = query_for(me, s)
     outgoing(n - 1).start()
+
+    def pass_on():
+        def wait_line(k, carry):
+            along_line(my_outer, lax.rem(my_outer + k, outer)).wait_recv()
+            return carry
+
+        lax.fori_loop(1, outer, wait_line, 0)
+
+        def start_block(k, carry):
+            inside_block(lax.rem(my_inner + k, inner), my_inner).start()
+            return carry
+
+        lax.fori_loop(1, inner, start_block, 0)
 
     for load in loads[4:]:
         load.wait()
@@ -199,66 +261,126 @@
         tokens_ref[r] = unit.astype(jnp.bfloat16)
         return carry
 
-    lax.fori_loop(0, rows, decode, 0)
+    lax.fori_loop(0, rows // 2, decode, 0)
+    pass_on()
+    lax.fori_loop(rows // 2, rows, decode, 0)
 
     gather_tokens = (lax.div(iota((CHUNK, CHUNK * qlen), 1), qlen) == iota((CHUNK, CHUNK * qlen), 0)).astype(jnp.bfloat16)
 
-    def back(offset):
+    def returning(position, owner, half, semaphores):
         return pltpu.make_async_remote_copy(
-            src_ref=scores_ref.at[offset],
-            dst_ref=returned_ref.at[me],
-            send_sem=back_send_sem.at[offset],
-            recv_sem=back_recv_sem.at[me],
-            device_id={AXIS: holder_of_mine(offset)},
+            src_ref=scores_ref.at[position, pl.ds(half * tile, tile)],
+            dst_ref=returned_ref.at[owner, pl.ds(half * tile, tile)],
+            send_sem=semaphores[0].at[position],
+            recv_sem=semaphores[1].at[owner],
+            device_id={AXIS: holder_of_mine(position)},
             device_id_type=pl.DeviceIdType.MESH,
         )
 
-    def send_back(offset, carry):
-        back(offset).start()
-        return carry
-
-    def add_up(i):
-        scored = split_dot(gather_tokens, maxima_ref[...], NT, True)
+    early = (back_send_sem, back_recv_sem)
+    late = (late_send_sem, late_recv_sem)
+
+    def send_back(position, carry):
+        returning(position, me, 0, early).start()
+        return carry
+
+    def send_late(position, carry):
+        returning(position, me, 1, late).start()
+        return carry
+
+    def add_up():
+        return split_dot(gather_tokens, maxima_ref[...], NT, True)
+
+    def keep_common(scored, first):
         for g in range(CHUNK):
-            at = i * CHUNK + g
-            scores_ref[lax.div(at, cap), pl.ds(lax.rem(at, cap), 1), pl.ds(0, rows)] = scored[g : g + 1, :]
-
-    def chunk(i, carry):
-        first = i * CHUNK
-        lax.fori_loop(lax.div(first - 1 + cap, cap), lax.div(first + CHUNK - 1, cap) + 1, wait_query_if, 0)
-        lax.fori_loop(jnp.maximum(done_before(i - 2), 1), jnp.maximum(done_before(i - 1), 1), send_back, 0)
-        add_up(jnp.maximum(i - 1, 0))
+            at = first + g
+            scores_ref[lax.div(at, cold), pl.ds(lax.rem(at, cold), 1), pl.ds(0, rows)] = scored[g : g + 1, :]
+
+    def keep_hot(scored, first):
+        for g in range(CHUNK):
+            at = first - common + g
+            place = lax.div(at, hot)
+            sender = lax.rem(place, outer) * inner + lax.div(place, outer)
+            away = lax.rem(me + n - sender, n)
+            position = jnp.where(away == 0, 0, lax.rem(away - n // 2 + n - 1, n - 1) + 1)
+            scores_ref[position, pl.ds(tile + lax.rem(at, hot), 1), pl.ds(0, rows)] = scored[g : g + 1, :]
+
+    def match(first):
         block = recv_ref[pl.ds(first, CHUNK)].reshape(CHUNK * qlen, dim)
         for r in range(rows):
             similar = dot(tokens_ref[r], block, NT)
             maxima_ref[r : r + 1, :] = jnp.max(similar, axis=0, keepdims=True)
+
+    def arrive(position, carry):
+        @pl.when(position >= 1)
+        def _():
+            outgoing(position).wait_recv()
+
         return carry
 
     def done_before(i):
-        return lax.div(jnp.maximum(i, 0) * CHUNK, cap)
-
-    def wait_query_if(offset, carry):
-        @pl.when(offset >= 1)
-        def _():
-            outgoing(offset).wait_recv()
-
-        return carry
-
-    lax.fori_loop(0, steps, chunk, 0)
-    add_up(steps - 1)
+        return lax.div(jnp.maximum(i, 0) * CHUNK, cold)
+
+    def common_chunk(i, carry):
+        first = i * CHUNK
+        lax.fori_loop(lax.div(first - 1 + cold, cold), lax.div(first + CHUNK - 1, cold) + 1, arrive, 0)
+        lax.fori_loop(jnp.maximum(done_before(i - 2), 1), jnp.maximum(done_before(i - 1), 1), send_back, 0)
+        if carry is None:
+            keep_hot(add_up(), n * cap - CHUNK)
+        else:
+            keep_common(add_up(), jnp.maximum(i - 1, 0) * CHUNK)
+        match(first)
+        return carry
+
+    def hot_chunk(i, carry):
+        keep_hot(add_up(), common + jnp.maximum(i - 1, 0) * CHUNK)
+        match(common + i * CHUNK)
+        return carry
+
+    lax.fori_loop(0, early_steps, common_chunk, 0)
+    keep_common(add_up(), (early_steps - 1) * CHUNK)
+
+    def wait_block(k, carry):
+        inside_block(my_inner, lax.rem(my_inner + k, inner)).wait_recv()
+        return carry
+
+    lax.fori_loop(1, inner, wait_block, 0)
+    lax.fori_loop(0, steps - common_steps, hot_chunk, 0)
+    common_chunk(early_steps, None)
+    lax.fori_loop(1, n, send_late, 0)
+    lax.fori_loop(early_steps + 1, common_steps, common_chunk, 0)
+    keep_common(add_up(), common - CHUNK)
 
     def wait_sent(offset, carry):
         outgoing(offset).wait_send()
         return carry
 
     lax.fori_loop(1, n, wait_sent, 0)
-    lax.fori_loop(max((steps - 2) * CHUNK // cap, 1), n, send_back, 0)
+    lax.fori_loop(max((common_steps - 2) * CHUNK // cold, 1), n, send_back, 0)
+
+    def line_sent(k, carry):
+        along_line(lax.rem(my_outer + k, outer), my_outer).wait_send()
+        return carry
+
+    lax.fori_loop(1, outer, line_sent, 0)
+
+    def block_sent(k, carry):
+        inside_block(lax.rem(my_inner + k, inner), my_inner).wait_send()
+        return carry
+
+    lax.fori_loop(1, inner, block_sent, 0)
     returned_ref[me] = scores_ref[0]
 
     spread = (lax.div(iota((LANES, n * padded), 1), padded) == iota((LANES, n * padded), 0)).astype(jnp.bfloat16)
     wide_slot = dot(slot_of, spread, NN)
     wide_iota = iota((count, n * padded), 1)
-    chosen = wide_slot == lax.rem(wide_iota, padded).astype(jnp.float32)
+    wide_place = lax.rem(wide_iota, padded)
+    wide_place = jnp.where(
+        wide_place < tile,
+        jnp.where(wide_place < cold, wide_place, -2),
+        jnp.where(wide_place < tile + hot, wide_place - tile + cold, -2),
+    )
+    chosen = wide_slot == wide_place.astype(jnp.float32)
     picks = jnp.concatenate(
         [
             jnp.where(chosen & (lax.div(wide_iota, padded * per_group) == g), 1.0, 0.0).astype(jnp.bfloat16)
@@ -267,16 +389,10 @@
         axis=0,
     )
 
-    def wait_back(offset, carry):
-        peer = partner(offset)
-        pltpu.make_async_remote_copy(
-            src_ref=scores_ref.at[offset],
-            dst_ref=returned_ref.at[peer],
-            send_sem=back_send_sem.at[offset],
-            recv_sem=back_recv_sem.at[peer],
-            device_id={AXIS: peer},
-            device_id_type=pl.DeviceIdType.MESH,
-        ).wait_recv()
+    def wait_back(position, carry):
+        owner = holder_of_mine(position)
+        returning(position, owner, 0, early).wait_recv()
+        returning(position, owner, 1, late).wait_recv()
         return carry
 
     lax.fori_loop(1, n, wait_back, 0)
@@ -293,7 +409,8 @@
     out_ref[...] = jnp.where(slot_iota < counted, result, 0.0)
 
     def wait_back_sent(offset, carry):
-        back(offset).wait_send()
+        returning(offset, me, 0, early).wait_send()
+        returning(offset, me, 1, late).wait_send()
         return carry
 
     lax.fori_loop(1, n, wait_back_sent, 0)
@@ -314,12 +431,14 @@
     slots = candidates.shape[1]
     rows, plen, _ = passage_base.shape
     cap = count * OWNERS_Q // n + 3
-    padded = -(-cap // 8) * 8
+    cold = -(-count * OWNERS_Q // n)
+    padded = 2 * (-(-max(cold, cap - cold) // 8) * 8)
+    inner = 1 << ((n.bit_length() - 1) // 2)
     total = placement_map.shape[0]
     vmem = pl.BlockSpec(memory_space=pltpu.VMEM)
     hbm = pl.BlockSpec(memory_space=pltpu.HBM)
     return pl.pallas_call(
-        functools.partial(kernel, n, cap),
+        functools.partial(kernel, n, cap, cold, inner),
         out_shape=jax.ShapeDtypeStruct((count, slots), jnp.float32),
         in_specs=[hbm] * 8,
         out_specs=vmem,
@@ -333,7 +452,7 @@
             pltpu.VMEM((rows, plen, dim), passage_base.dtype),
             pltpu.VMEM((rows, plen, dim), jnp.int32),
             pltpu.VMEM((rows, plen, dim), jnp.bfloat16),
-            pltpu.VMEM((n * cap, qlen, dim), jnp.bfloat16),
+            pltpu.VMEM((n * cold, qlen, dim), jnp.bfloat16),
             pltpu.VMEM((n * cap, qlen, dim), jnp.bfloat16),
             pltpu.VMEM((n, LANES), jnp.int32),
             pltpu.SMEM((n, LANES), jnp.int32),
@@ -344,6 +463,12 @@
             pltpu.SemaphoreType.DMA,
             pltpu.SemaphoreType.DMA((n,)),
             pltpu.SemaphoreType.DMA((n,)),
+            pltpu.SemaphoreType.DMA((n,)),
+            pltpu.SemaphoreType.DMA((n,)),
+            pltpu.SemaphoreType.DMA((n // inner,)),
+            pltpu.SemaphoreType.DMA((n // inner,)),
+            pltpu.SemaphoreType.DMA((inner,)),
+            pltpu.SemaphoreType.DMA((inner,)),
             pltpu.SemaphoreType.DMA((n,)),
             pltpu.SemaphoreType.DMA((n,)),
         ],

time: 47.8 us -> 44.2 us (0.925)
  Pallas kernels: 46.1 us -> 42.5 us
    pallas_call x1, Pallas kernels: 46.1 us -> 42.5 us  [local(): pl.pallas_call(functools.partial(kernel, n, cap, cold, inner), out_shape=...]
where the time goes in v3:
time: 44.2 us; the launch traced here: 43.9 us
  Pallas kernels  42.5 us (96%)
  local copies, waits for them, and re-layouts  1.39 us (3%)
    pallas_call x1, Pallas kernels, local(): pl.pallas_call(functools.partial(kernel, n, cap, cold, inner), out_shape=...  42.5 us
    pallas_call x1, local copies, waits for them, and re-layouts, local(): pl.pallas_call(functools.partial(kernel, n, cap, cold, inner), out_shape=...  1.39 us

profile of v3, /device:TPU:0, one launch (start us, length us, event | category | flops | bytes accessed | tf_op | source)
XLA Modules:
  0.0 43.9 jit_solution(13402335823086259104)
XLA Ops:
  0.0 42.5 %rerank.1 = f32[32,24]{1,0:T(8,128)} custom-call(f32[1,4]{1,0:T(1,128)} %bitcast.7, s32[1,32]{1,0:T(1,128)} %bitcast.8, bf16[32,32,128]{2,1,0:T(8,128)(2,1)} %queries_hbm.1, s32[24,32]{1,0:T(8,128)} %bitcast.5, s32[1,32]{1,0:T(1,128)} %bitcast.9, s32[1,512]{1,0:T(1,128)} %bitcast.6, bf16[32,128,128]{2,1,0:T(8,128)(2,1)} %base_hbm.1, s32[32,128,128]{2,1,0:T(8,128)} %codes_hbm.1), custom_call_target="tpu_custom_call" | custom-call | tf_op jit(solution)/shard_map/rerank/pallas_call | solution.py:440
  42.5 1.4 %copy.9 = f32[32,24]{0,1:T(8,128)} copy(f32[32,24]{1,0:T(8,128)} %rerank.1) | data formatting | bytes 6144 | tf_op jit(solution)/shard_map/rerank/pallas_call | solution.py:440

commit v4 on v3

--- a/solution.py
+++ b/solution.py
@@ -8,7 +8,7 @@
 from jax.sharding import PartitionSpec as P
 
 OWNERS_Q = 3
-CHUNK = 8
+CHUNK = 16
 LANES = 128
 EPSILON = 1e-06
 AXIS = "shard"
@@ -90,12 +90,12 @@
     common = n * cold
     common_steps = common // CHUNK
     steps = n * cap // CHUNK
-    early_steps = common_steps * 2 // 3
+    early_steps = common_steps // 3
     my_outer, my_inner = lax.div(me, inner), lax.rem(me, inner)
     tile = padded // 2
 
     def shift(position):
-        return jnp.where(position == 0, 0, lax.rem(position + n // 2 - 2 + n - 1, n - 1) + 1)
+        return position
 
     def partner(position):
         return lax.rem(me + shift(position), n)
@@ -261,9 +261,9 @@
         tokens_ref[r] = unit.astype(jnp.bfloat16)
         return carry
 
-    lax.fori_loop(0, rows // 2, decode, 0)
+    lax.fori_loop(0, rows // 2, decode, 0, unroll=2)
     pass_on()
-    lax.fori_loop(rows // 2, rows, decode, 0)
+    lax.fori_loop(rows // 2, rows, decode, 0, unroll=2)
 
     gather_tokens = (lax.div(iota((CHUNK, CHUNK * qlen), 1), qlen) == iota((CHUNK, CHUNK * qlen), 0)).astype(jnp.bfloat16)
 
@@ -291,19 +291,24 @@
     def add_up():
         return split_dot(gather_tokens, maxima_ref[...], NT, True)
 
+    def walk(first, size):
+        whole = lax.div(first, size)
+        rest = first - whole * size
+        for g in range(CHUNK):
+            yield g, whole, rest
+            full = rest + 1 == size
+            whole = jnp.where(full, whole + 1, whole)
+            rest = jnp.where(full, 0, rest + 1)
+
     def keep_common(scored, first):
-        for g in range(CHUNK):
-            at = first + g
-            scores_ref[lax.div(at, cold), pl.ds(lax.rem(at, cold), 1), pl.ds(0, rows)] = scored[g : g + 1, :]
+        for g, position, slot in walk(first, cold):
+            scores_ref[position, pl.ds(slot, 1), pl.ds(0, rows)] = scored[g : g + 1, :]
 
     def keep_hot(scored, first):
-        for g in range(CHUNK):
-            at = first - common + g
-            place = lax.div(at, hot)
+        for g, place, slot in walk(first - common, hot):
             sender = lax.rem(place, outer) * inner + lax.div(place, outer)
-            away = lax.rem(me + n - sender, n)
-            position = jnp.where(away == 0, 0, lax.rem(away - n // 2 + n - 1, n - 1) + 1)
-            scores_ref[position, pl.ds(tile + lax.rem(at, hot), 1), pl.ds(0, rows)] = scored[g : g + 1, :]
+            position = jnp.where(sender > me, me + n - sender, me - sender)
+            scores_ref[position, pl.ds(tile + slot, 1), pl.ds(0, rows)] = scored[g : g + 1, :]
 
     def match(first):
         block = recv_ref[pl.ds(first, CHUNK)].reshape(CHUNK * qlen, dim)

time: 44.2 us -> 40.6 us (0.919)
  Pallas kernels: 42.5 us -> 38.9 us
    pallas_call x1, Pallas kernels: 42.5 us -> 38.9 us  [local(): pl.pallas_call(functools.partial(kernel, n, cap, cold, inner), out_shape=...]
where the time goes in v4:
time: 40.6 us; the launch traced here: 40.3 us
  Pallas kernels  38.9 us (96%)
  local copies, waits for them, and re-layouts  1.39 us (3%)
    pallas_call x1, Pallas kernels, local(): pl.pallas_call(functools.partial(kernel, n, cap, cold, inner), out_shape=...  38.9 us
    pallas_call x1, local copies, waits for them, and re-layouts, local(): pl.pallas_call(functools.partial(kernel, n, cap, cold, inner), out_shape=...  1.39 us

profile of v4, /device:TPU:0, one launch (start us, length us, event | category | flops | bytes accessed | tf_op | source)
XLA Modules:
  0.0 40.3 jit_solution(3827999506347435953)
XLA Ops:
  0.0 38.9 %rerank.1 = f32[32,24]{1,0:T(8,128)} custom-call(f32[1,4]{1,0:T(1,128)} %bitcast.7, s32[1,32]{1,0:T(1,128)} %bitcast.8, bf16[32,32,128]{2,1,0:T(8,128)(2,1)} %queries_hbm.1, s32[24,32]{1,0:T(8,128)} %bitcast.5, s32[1,32]{1,0:T(1,128)} %bitcast.9, s32[1,512]{1,0:T(1,128)} %bitcast.6, bf16[32,128,128]{2,1,0:T(8,128)(2,1)} %base_hbm.1, s32[32,128,128]{2,1,0:T(8,128)} %codes_hbm.1), custom_call_target="tpu_custom_call" | custom-call | tf_op jit(solution)/shard_map/rerank/pallas_call | solution.py:445
  38.9 1.4 %copy.9 = f32[32,24]{0,1:T(8,128)} copy(f32[32,24]{1,0:T(8,128)} %rerank.1) | data formatting | bytes 6144 | tf_op jit(solution)/shard_map/rerank/pallas_call | solution.py:445
